TPU v7x, 32 devices: a whole 2x2x4 slice. The times are simulated.
32 devices in a mesh: wide: 8 (over y, x, core), narrow: 4 (over z).
Axes of the slice: x: 2, y: 2, z: 4, core: 2. Of those that a mesh axis runs over, the one named last changes fastest.
Arguments:
- sources: bfloat16 [2, 1024, 8192], P(None, None, ('wide', 'narrow')), may hold values from -6 to 6
- leaf_in: bfloat16 [2, 128, 64, 64], P(None, ('wide', 'narrow')), may hold values from -0.75 to 0.75
- transfer: bfloat16 [7, 2, 128, 64, 128], P(None, None, ('wide', 'narrow')), may hold values from -0.5 to 0.5
- leaf_out: bfloat16 [2, 128, 64, 64], P(None, ('wide', 'narrow')), may hold values from -0.75 to 0.75
Outputs:
- targets: bfloat16 [2, 1024, 8192], P(None, None, ('wide', 'narrow'))
All inputs are finite; a program needn't handle non-finite values.
Results may differ from a plain program's by a relative error of at most 0.0095.
Values may be sent and summed in bfloat16 or wider, within the bound.
A program may use at most 64 MiB of HBM per device.

v0:
```python
import jax
import jax.numpy as jnp
from jax import lax
from jax.sharding import PartitionSpec as P


def partner_2(value, axis, apart):
    return lax.ppermute(value, axis, [(i, i ^ 1 << apart) for i in range(lax.axis_size(axis))])


def local_partner(coef, bit, rank):
    halves, rows, cols = coef.shape
    blocks = cols // rank
    grouped = coef.reshape(halves, rows, blocks // (2 << bit), 2, (1 << bit) * rank)
    return grouped[:, :, :, ::-1].reshape(halves, rows, cols)


def mix_level(coef, partner, weight):
    halves, rows, cols = coef.shape
    blocks = weight.shape[1]
    rank = weight.shape[2]
    joined = jnp.concatenate(
        [coef.reshape(halves, rows, blocks, rank), partner.reshape(halves, rows, blocks, rank)],
        axis=-1,
    )
    mixed = jnp.einsum("hakj,hkoj->hako", joined, weight, preferred_element_type=jnp.float32)
    return mixed.astype(jnp.bfloat16).reshape(halves, rows, cols)


def wide_level(coef, weight, bit):
    partner = partner_2(coef, "wide", bit)
    return mix_level(coef, partner, weight)


def shards(sources, leaf_in, transfer, leaf_out):
    halves, rows, cols = sources.shape
    blocks = leaf_in.shape[1]
    leaf = leaf_in.shape[2]
    rank = leaf_in.shape[3]
    local_bits = blocks.bit_length() - 1
    narrow_bits = lax.axis_size("narrow").bit_length() - 1
    wide_bits = lax.axis_size("wide").bit_length() - 1
    points_in = sources[::-1].reshape(halves, rows, blocks, leaf)
    coef = jnp.einsum("hakm,hkmr->hakr", points_in, leaf_in, preferred_element_type=jnp.float32)
    coef = coef.astype(jnp.bfloat16).reshape(halves, rows, blocks * rank)
    for level in range(local_bits):
        coef = mix_level(coef, local_partner(coef, level, rank), transfer[level])
    for bit in range(narrow_bits):
        partner = partner_2(coef, "narrow", bit)
        coef = mix_level(coef, partner, transfer[local_bits + bit])
    first_wide = local_bits + narrow_bits
    for bit in range(wide_bits):
        coef = wide_level(coef, transfer[first_wide + bit], bit)
    images = jnp.einsum(
        "hakr,hkrm->hakm",
        coef.reshape(halves, rows, blocks, rank),
        leaf_out,
        preferred_element_type=jnp.float32,
    )
    return images.astype(jnp.bfloat16).reshape(halves, rows, blocks * leaf)


def solution(mesh):
    return jax.shard_map(
        shards,
        mesh=mesh,
        in_specs=(
            P(None, None, ("wide", "narrow")),
            P(None, ("wide", "narrow"), None, None),
            P(None, None, ("wide", "narrow"), None, None),
            P(None, ("wide", "narrow"), None, None),
        ),
        out_specs=P(None, None, ("wide", "narrow")),
        check_vma=False,
    )
```

profile of v0, /device:TPU:0, one launch (start us, length us, event | category | flops | bytes accessed | tf_op | source)
XLA Modules:
  0.0 136.3 jit_solution(357174921053192285)
XLA Ops:
  0.0 0.0 copy-start
  0.0 1.5 %copy.15 = bf16[2,1024,256]{1,2,0:T(8,128)(2,1)S(1)} copy(bf16[2,1024,256]{2,1,0:T(8,128)(2,1)} %param.4) | data formatting | bytes 2097152 | tf_op args[0]
  1.5 0.1 rev.9
  1.6 0.0 copy-done
  1.6 0.5 convolution_convert_fusion.1
  2.1 0.1 rev.10
  2.2 1.3 fusion.46
  3.5 0.0 copy-start.1
  3.5 0.1 rev.11
  3.6 1.1 copy-done.1
  4.7 0.4 fusion.43
  5.1 3.1 %collective-permute-start = (bf16[2,1024,256]{1,2,0:T(8,128)(2,1)S(1)}, bf16[2,1024,256]{1,2,0:T(8,128)(2,1)S(1)}, u32[]{:S(2)}, u32[]{:S(2)}) collective-permute-start(bf16[2,1024,256]{1,2,0:T(8,128)(2,1)S(1)} %bitcast.69), channel_id=1, source_target_pairs={{0,1},{1,0},{2,3},{3,2},{4,5},{5,4},{6,7},{7,6},{8,9},{9,8},{10,11... | collective-permute-start | bytes 3145736 | tf_op jit(solution)/shard_map/ppermute | solution.py:8
  8.3 23.2 %collective-permute-done = bf16[2,1024,256]{1,2,0:T(8,128)(2,1)S(1)} collective-permute-done((bf16[2,1024,256]{1,2,0:T(8,128)(2,1)S(1)}, bf16[2,1024,256]{1,2,0:T(8,128)(2,1)S(1)}, u32[]{:S(2)}, u32[]{:S(2)}) %collective-permute-start) | collective-permute-done | bytes 1048608 | tf_op jit(solution)/shard_map/ppermute | solution.py:8
  31.4 0.4 fusion.40
  31.9 2.8 %collective-permute-start.1 = (bf16[2,1024,256]{1,2,0:T(8,128)(2,1)S(1)}, bf16[2,1024,256]{1,2,0:T(8,128)(2,1)S(1)}, u32[]{:S(2)}, u32[]{:S(2)}) collective-permute-start(bf16[2,1024,256]{1,2,0:T(8,128)(2,1)S(1)} %bitcast.71), channel_id=1, source_target_pairs={{0,2},{1,3},{2,0},{3,1},{4,6},{5,7},{6,4},{7,5},{8,10},{9,11},{10,... | collective-permute-start | bytes 3145736 | tf_op jit(solution)/shard_map/ppermute | solution.py:8
  34.7 44.9 %collective-permute-done.1 = bf16[2,1024,256]{1,2,0:T(8,128)(2,1)S(1)} collective-permute-done((bf16[2,1024,256]{1,2,0:T(8,128)(2,1)S(1)}, bf16[2,1024,256]{1,2,0:T(8,128)(2,1)S(1)}, u32[]{:S(2)}, u32[]{:S(2)}) %collective-permute-start.1) | collective-permute-done | bytes 1048608 | tf_op jit(solution)/shard_map/ppermute | solution.py:8
  79.6 0.4 fusion.37
  80.1 0.1 collective-permute-start.2
  80.1 2.6 %collective-permute-done.2 = bf16[2,1024,256]{1,2,0:T(8,128)(2,1)S(1)} collective-permute-done((bf16[2,1024,256]{1,2,0:T(8,128)(2,1)S(1)}, bf16[2,1024,256]{1,2,0:T(8,128)(2,1)S(1)}, u32[]{:S(2)}, u32[]{:S(2)}) %collective-permute-start.2) | collective-permute-done | bytes 1048608 | tf_op jit(solution)/shard_map/ppermute | solution.py:8
  82.8 0.4 fusion.34
  83.2 1.4 %collective-permute-start.3 = (bf16[2,1024,256]{1,2,0:T(8,128)(2,1)S(1)}, bf16[2,1024,256]{1,2,0:T(8,128)(2,1)S(1)}, u32[]{:S(2)}, u32[]{:S(2)}) collective-permute-start(bf16[2,1024,256]{1,2,0:T(8,128)(2,1)S(1)} %bitcast.75), channel_id=1, source_target_pairs={{0,8},{4,12},{8,0},{12,4},{16,24},{20,28},{24,16},{28,20},{1,9},{5... | collective-permute-start | bytes 3145736 | tf_op jit(solution)/shard_map/ppermute | solution.py:8
  84.7 23.8 %collective-permute-done.3 = bf16[2,1024,256]{1,2,0:T(8,128)(2,1)S(1)} collective-permute-done((bf16[2,1024,256]{1,2,0:T(8,128)(2,1)S(1)}, bf16[2,1024,256]{1,2,0:T(8,128)(2,1)S(1)}, u32[]{:S(2)}, u32[]{:S(2)}) %collective-permute-start.3) | collective-permute-done | bytes 1048608 | tf_op jit(solution)/shard_map/ppermute | solution.py:8
  108.5 0.0 copy-start.2
  108.5 0.4 fusion.31
  108.9 1.5 %collective-permute-start.4 = (bf16[2,1024,256]{1,2,0:T(8,128)(2,1)S(1)}, bf16[2,1024,256]{1,2,0:T(8,128)(2,1)S(1)}, u32[]{:S(2)}, u32[]{:S(2)}) collective-permute-start(bf16[2,1024,256]{1,2,0:T(8,128)(2,1)S(1)} %bitcast.77), channel_id=1, source_target_pairs={{0,16},{4,20},{8,24},{12,28},{16,0},{20,4},{24,8},{28,12},{1,17},{... | collective-permute-start | bytes 3145736 | tf_op jit(solution)/shard_map/ppermute | solution.py:8
  110.4 22.9 %collective-permute-done.4 = bf16[2,1024,256]{1,2,0:T(8,128)(2,1)S(1)} collective-permute-done((bf16[2,1024,256]{1,2,0:T(8,128)(2,1)S(1)}, bf16[2,1024,256]{1,2,0:T(8,128)(2,1)S(1)}, u32[]{:S(2)}, u32[]{:S(2)}) %collective-permute-start.4) | collective-permute-done | bytes 1048608 | tf_op jit(solution)/shard_map/ppermute | solution.py:8
  133.3 0.0 copy-done.2
  133.4 1.6 %convolution_convert_fusion = bf16[2,4,1024,64]{2,3,1,0:T(8,128)(2,1)S(1)} fusion(bf16[2,4,64,64]{3,2,1,0:T(8,128)(2,1)S(1)} %copy-done.2, bf16[2,1024,4,64]{1,3,2,0:T(8,128)(2,1)S(1)} %bitcast.83, bf16[2,1024,4,64]{1,3,2,0:T(8,128)(2,1)S(1)} %bitcast.78, bf16[7,2,4,64,128]{4,3,2,1,0:T(8,128)(2,1)} %param.6), kind=kOutput, calls=%fused_computation.35 | convolution fusion | flops 206569472 | bytes 3342336 | tf_op jit(solution)/shard_map/hakr,hkrm->hakm/dot_general | solution.py:54
  135.0 1.3 copy.24
Async XLA Ops:
  0.0 1.6 %copy-start = (bf16[2,4,64,64]{3,2,1,0:T(8,128)(2,1)S(1)}, bf16[2,4,64,64]{3,2,1,0:T(8,128)(2,1)}, u32[]{:S(2)}) copy-start(bf16[2,4,64,64]{3,2,1,0:T(8,128)(2,1)} %param.5) | copy-start | bytes 196612
  3.5 1.2 copy-start.1
  5.1 26.3 %collective-permute-start = (bf16[2,1024,256]{1,2,0:T(8,128)(2,1)S(1)}, bf16[2,1024,256]{1,2,0:T(8,128)(2,1)S(1)}, u32[]{:S(2)}, u32[]{:S(2)}) collective-permute-start(bf16[2,1024,256]{1,2,0:T(8,128)(2,1)S(1)} %bitcast.69), channel_id=1, source_target_pairs={{0,1},{1,0},{2,3},{3,2},{4,5},{5,4},{6,7},{7,6},{8,9},{9,8},{10,11... | collective-permute-start | bytes 3145736 | tf_op jit(solution)/shard_map/ppermute | solution.py:8
  31.9 47.8 %collective-permute-start.1 = (bf16[2,1024,256]{1,2,0:T(8,128)(2,1)S(1)}, bf16[2,1024,256]{1,2,0:T(8,128)(2,1)S(1)}, u32[]{:S(2)}, u32[]{:S(2)}) collective-permute-start(bf16[2,1024,256]{1,2,0:T(8,128)(2,1)S(1)} %bitcast.71), channel_id=1, source_target_pairs={{0,2},{1,3},{2,0},{3,1},{4,6},{5,7},{6,4},{7,5},{8,10},{9,11},{10,... | collective-permute-start | bytes 3145736 | tf_op jit(solution)/shard_map/ppermute | solution.py:8
  80.1 2.7 %collective-permute-start.2 = (bf16[2,1024,256]{1,2,0:T(8,128)(2,1)S(1)}, bf16[2,1024,256]{1,2,0:T(8,128)(2,1)S(1)}, u32[]{:S(2)}, u32[]{:S(2)}) collective-permute-start(bf16[2,1024,256]{1,2,0:T(8,128)(2,1)S(1)} %bitcast.73), channel_id=1, source_target_pairs={{0,4},{4,0},{8,12},{12,8},{16,20},{20,16},{24,28},{28,24},{1,5},{5... | collective-permute-start | bytes 3145736 | tf_op jit(solution)/shard_map/ppermute | solution.py:8
  83.2 25.3 %collective-permute-start.3 = (bf16[2,1024,256]{1,2,0:T(8,128)(2,1)S(1)}, bf16[2,1024,256]{1,2,0:T(8,128)(2,1)S(1)}, u32[]{:S(2)}, u32[]{:S(2)}) collective-permute-start(bf16[2,1024,256]{1,2,0:T(8,128)(2,1)S(1)} %bitcast.75), channel_id=1, source_target_pairs={{0,8},{4,12},{8,0},{12,4},{16,24},{20,28},{24,16},{28,20},{1,9},{5... | collective-permute-start | bytes 3145736 | tf_op jit(solution)/shard_map/ppermute | solution.py:8
  108.5 24.9 %copy-start.2 = (bf16[2,4,64,64]{3,2,1,0:T(8,128)(2,1)S(1)}, bf16[2,4,64,64]{3,2,1,0:T(8,128)(2,1)}, u32[]{:S(2)}) copy-start(bf16[2,4,64,64]{3,2,1,0:T(8,128)(2,1)} %param.7) | copy-start | bytes 196612
  108.9 24.4 %collective-permute-start.4 = (bf16[2,1024,256]{1,2,0:T(8,128)(2,1)S(1)}, bf16[2,1024,256]{1,2,0:T(8,128)(2,1)S(1)}, u32[]{:S(2)}, u32[]{:S(2)}) collective-permute-start(bf16[2,1024,256]{1,2,0:T(8,128)(2,1)S(1)} %bitcast.77), channel_id=1, source_target_pairs={{0,16},{4,20},{8,24},{12,28},{16,0},{20,4},{24,8},{28,12},{1,17},{... | collective-permute-start | bytes 3145736 | tf_op jit(solution)/shard_map/ppermute | solution.py:8
where the time goes:
time: 136 us
  waiting for transfers between devices  118 us (87%)
  starting transfers between devices  8.92 us (7%)
  matrix products  5.58 us (4%)
  local copies, waits for them, and re-layouts  4.14 us (3%)
    ppermute x5, waiting for transfers between devices, partner_2(): lax.ppermute(value, axis, [(i, i ^ 1 << apart) for i in range(lax.axis_si...  118 us
    ppermute x5, starting transfers between devices, partner_2(): lax.ppermute(value, axis, [(i, i ^ 1 << apart) for i in range(lax.axis_si...  8.92 us
    dot_general x6, matrix products, mix_level(): jnp.einsum('hakj,hkoj->hako', joined, weight, preferred_element_type=jnp....  3.5 us
  transfers between devices with their start and end apart: 5, of which 5 were waited for; matrix products, arithmetic and copies ran while one was open for 0% of the time, Pallas kernels for 0%

commit v1 on v0

v1 whole, which is shorter than its diff:
```python
import functools

import jax
import jax.numpy as jnp
from jax import lax
from jax.experimental import pallas as pl
from jax.experimental.pallas import tpu as pltpu
from jax.sharding import PartitionSpec as P

MESH = pl.DeviceIdType.MESH
CHUNK_ROWS = 128
FIRST_GAPS = (2, 2)
GAP = 1


def dot_nt(x, w):
    return lax.dot_general(x, w, (((1,), (1,)), ((), ())), preferred_element_type=jnp.float32)


def dot_nn(x, w):
    return lax.dot_general(x, w, (((1,), (0,)), ((), ())), preferred_element_type=jnp.float32)


def spread(tile, half, lanes_half):
    wide = tile.astype(jnp.float32)
    width = wide.shape[1] // 2
    if half != lanes_half:
        wide = pltpu.roll(wide, width, 1)
    lane = lax.broadcasted_iota(jnp.int32, wide.shape, 1)
    keep = lane < width if lanes_half == 0 else lane >= width
    return jnp.where(keep, wide, 0.0).astype(jnp.bfloat16)


def kernel(
    dims, src, leaf_in, transfer, leaf_out, out,
    src_v, in_v, tr_v, out_w_v, w_in, w_loc, w_own, w_par, w_out, held, got, res,
    src_sem, w_sem, out_sem, send_sem, recv_sem,
):
    local_bits, narrow_bits, wide_bits, blocks, rank, chunks, rows, halves = dims
    exchanges = narrow_bits + wide_bits
    cols = blocks * rank

    partners = []
    for axis, bits in (("narrow", narrow_bits), ("wide", wide_bits)):
        me = lax.axis_index(axis)
        for bit in range(bits):
            step = 1 << bit
            flag = lax.rem(lax.div(me, step), 2)
            partners.append({axis: me + step * (1 - 2 * flag)})

    barrier = pltpu.get_barrier_semaphore()
    for partner in partners:
        pl.semaphore_signal(barrier, inc=1, device_id=partner, device_id_type=MESH)

    def rows_of(c):
        return lax.rem(c, halves), pl.ds(pl.multiple_of(lax.div(c, halves) * rows, rows), rows)

    def src_copy(c):
        h, r = rows_of(c)
        return pltpu.make_async_copy(src.at[halves - 1 - h, r], src_v.at[c], src_sem.at[c])

    def out_copy(c):
        h, r = rows_of(c)
        return pltpu.make_async_copy(res.at[c], out.at[h, r], out_sem.at[c])

    in_copy = pltpu.make_async_copy(leaf_in, in_v, w_sem.at[0])
    loc_copy = pltpu.make_async_copy(transfer.at[pl.ds(0, local_bits)], tr_v.at[pl.ds(0, local_bits)], w_sem.at[1])
    ex_copy = pltpu.make_async_copy(transfer.at[pl.ds(local_bits, exchanges)], tr_v.at[pl.ds(local_bits, exchanges)], w_sem.at[2])
    last_copy = pltpu.make_async_copy(leaf_out, out_w_v, w_sem.at[3])
    in_copy.start()
    loc_copy.start()
    lax.fori_loop(0, chunks, lambda c, _: (src_copy(c).start(), None)[1], None)
    ex_copy.start()
    last_copy.start()

    def leaf_build(dst, leaf):
        dst[...] = jnp.zeros_like(dst)
        for h in range(halves):
            for k in range(blocks):
                w = leaf[h, k]
                tile = jnp.concatenate([w, w], axis=1)
                at = k * rank // (2 * rank) * 2 * rank
                dst[h, k * rank:(k + 1) * rank, at:at + 2 * rank] = spread(tile, k % 2, k % 2)

    in_copy.wait()
    leaf_build(w_in, in_v)
    loc_copy.wait()
    w_loc[...] = jnp.zeros_like(w_loc)
    for level in range(local_bits):
        for h in range(halves):
            for k in range(blocks):
                w = tr_v[level, h, k]
                p = k ^ (1 << level)
                r = slice(k * rank, (k + 1) * rank)
                own = spread(w, 0, k % 2)
                par = spread(w, 1, p % 2)
                ka, pa = k // 2 * 2 * rank, p // 2 * 2 * rank
                if ka == pa:
                    w_loc[level, h, r, ka:ka + 2 * rank] = own + par
                else:
                    w_loc[level, h, r, ka:ka + 2 * rank] = own
                    w_loc[level, h, r, pa:pa + 2 * rank] = par

    def send(e, c):
        return pltpu.make_async_remote_copy(
            src_ref=held.at[e, c],
            dst_ref=got.at[e, c],
            send_sem=send_sem.at[e, c],
            recv_sem=recv_sem.at[e, c],
            device_id=partners[e],
            device_id_type=MESH,
        )

    def first(c):
        h, _ = rows_of(c)
        src_copy(c).wait()
        x = dot_nn(src_v[c], w_in[h]).astype(jnp.bfloat16)
        for level in range(local_bits):
            x = dot_nt(x, w_loc[level, h]).astype(jnp.bfloat16)
        held[0, c] = x

    def mix(e, c):
        h, _ = rows_of(c)
        acc = dot_nt(held[e, c], w_own[e, h])
        send(e, c).wait_recv()
        acc = acc + dot_nt(got[e, c], w_par[e, h])
        x = acc.astype(jnp.bfloat16)
        if e + 1 < exchanges:
            held[e + 1, c] = x
            send(e + 1, c).start()
        else:
            res[c] = dot_nn(x, w_out[h]).astype(jnp.bfloat16)
            out_copy(c).start()

    gaps = list(FIRST_GAPS[:exchanges]) + [GAP] * (exchanges - len(FIRST_GAPS))
    after = [sum(gaps[:e + 1]) for e in range(exchanges)]
    lead = after[0]

    first(0)
    pl.semaphore_wait(barrier, len(partners))
    send(0, 0).start()

    def ahead(c, _):
        first(c)
        send(0, c).start()

    lax.fori_loop(1, lead, ahead, None)

    ex_copy.wait()
    w_own[...] = jnp.zeros_like(w_own)
    w_par[...] = jnp.zeros_like(w_par)
    for e in range(exchanges):
        for h in range(halves):
            for k in range(blocks):
                w = tr_v[local_bits + e, h, k]
                r = slice(k * rank, (k + 1) * rank)
                at = k // 2 * 2 * rank
                w_own[e, h, r, at:at + 2 * rank] = spread(w, 0, k % 2)
                w_par[e, h, r, at:at + 2 * rank] = spread(w, 1, k % 2)
    last_copy.wait()
    leaf_build(w_out, out_w_v)

    def step(t, _):
        for e in range(exchanges):
            c = t - after[e]
            if e == 1:
                @pl.when(t < chunks)
                def _():
                    first(t)
                    send(0, t).start()

            @pl.when((c >= 0) & (c < chunks))
            def _(e=e, c=c):
                mix(e, c)

    lax.fori_loop(lead, chunks + after[-1], step, None)

    def finish(c, _):
        out_copy(c).wait()
        for e in range(exchanges):
            send(e, c).wait_send()

    lax.fori_loop(0, chunks, finish, None)


def shards(sources, leaf_in, transfer, leaf_out):
    halves, points_rows, cols = sources.shape
    blocks, leaf, rank = leaf_in.shape[1:]
    levels = transfer.shape[0]
    local_bits = blocks.bit_length() - 1
    narrow_bits = lax.axis_size("narrow").bit_length() - 1
    wide_bits = lax.axis_size("wide").bit_length() - 1
    exchanges = narrow_bits + wide_bits
    rows = CHUNK_ROWS
    chunks = halves * points_rows // rows
    dims = (local_bits, narrow_bits, wide_bits, blocks, rank, chunks, rows, halves)
    bf = jnp.bfloat16
    any_spec = pl.BlockSpec(memory_space=pl.ANY)
    return pl.pallas_call(
        functools.partial(kernel, dims),
        out_shape=jax.ShapeDtypeStruct(sources.shape, bf),
        in_specs=[any_spec] * 4,
        out_specs=any_spec,
        scratch_shapes=[
            pltpu.VMEM((chunks, rows, cols), bf),
            pltpu.VMEM(leaf_in.shape, bf),
            pltpu.VMEM(transfer.shape, bf),
            pltpu.VMEM(leaf_out.shape, bf),
            pltpu.VMEM((halves, cols, cols), bf),
            pltpu.VMEM((local_bits, halves, cols, cols), bf),
            pltpu.VMEM((exchanges, halves, cols, cols), bf),
            pltpu.VMEM((exchanges, halves, cols, cols), bf),
            pltpu.VMEM((halves, cols, cols), bf),
            pltpu.VMEM((exchanges, chunks, rows, cols), bf),
            pltpu.VMEM((exchanges, chunks, rows, cols), bf),
            pltpu.VMEM((chunks, rows, cols), bf),
            pltpu.SemaphoreType.DMA((chunks,)),
            pltpu.SemaphoreType.DMA((4,)),
            pltpu.SemaphoreType.DMA((chunks,)),
            pltpu.SemaphoreType.DMA((exchanges, chunks)),
            pltpu.SemaphoreType.DMA((exchanges, chunks)),
        ],
        compiler_params=pltpu.CompilerParams(
            collective_id=0, has_side_effects=True, vmem_limit_bytes=60 * 1024 * 1024
        ),
    )(sources, leaf_in, transfer, leaf_out)


def solution(mesh):
    return jax.shard_map(
        shards,
        mesh=mesh,
        in_specs=(
            P(None, None, ("wide", "narrow")),
            P(None, ("wide", "narrow"), None, None),
            P(None, None, ("wide", "narrow"), None, None),
            P(None, ("wide", "narrow"), None, None),
        ),
        out_specs=P(None, None, ("wide", "narrow")),
        check_vma=False,
    )
```

time: 136 us -> 73.1 us (0.54)
  waiting for transfers between devices: 118 us -> 0 us
  Pallas kernels: 0 us -> 70.7 us
  starting transfers between devices: 8.92 us -> 0 us
  matrix products: 5.58 us -> 0 us
  local copies, waits for them, and re-layouts: 4.14 us -> 2.26 us
    ppermute x5 -> x0, waiting for transfers between devices: 118 us -> none  [partner_2(): lax.ppermute(value, axis, [(i, i ^ 1 << apart) for i in range(lax.axis_si...]
    pallas_call x0 -> x1, Pallas kernels: none -> 70.7 us  [shards(): pl.pallas_call(functools.partial(kernel, dims), out_shape=jax.ShapeDtypeS...]
    ppermute x5 -> x0, starting transfers between devices: 8.92 us -> none  [partner_2(): lax.ppermute(value, axis, [(i, i ^ 1 << apart) for i in range(lax.axis_si...]
    dot_general x8 -> x0, matrix products: 5.58 us -> none  [the longest x6 3.5 us: mix_level(): jnp.einsum('hakj,hkoj->hako', joined, weight, preferred_element_type=jnp....]
  transfers between devices with their start and end apart: 5 -> 0, of which waited for: 5 -> 0; matrix products, arithmetic and copies ran while one was open for 0% -> 0% of each run, Pallas kernels for 0% -> 0%
where the time goes in v1:
time: 73.1 us; the launch traced here: 73 us
  Pallas kernels  70.7 us (97%)
  local copies, waits for them, and re-layouts  2.26 us (3%)
    pallas_call x1, Pallas kernels, shards(): pl.pallas_call(functools.partial(kernel, dims), out_shape=jax.ShapeDtypeS...  70.7 us
    unnamed x1, local copies, waits for them, and re-layouts  2.26 us

profile of v1, /device:TPU:0, one launch (start us, length us, event | category | flops | bytes accessed | tf_op | source)
XLA Modules:
  0.0 73.0 jit_solution(3768422207254128705)
XLA Ops:
  0.0 70.7 %shard_map.46 = bf16[2,1024,256]{2,1,0:T(8,128)(2,1)} custom-call(bf16[2,1024,256]{2,1,0:T(8,128)(2,1)} %src.1, bf16[2,4,64,64]{3,2,1,0:T(8,128)(2,1)} %leaf_in.1, bf16[7,2,4,64,128]{4,3,2,1,0:T(8,128)(2,1)} %transfer.1, bf16[2,4,64,64]{3,2,1,0:T(8,128)(2,1)} %leaf_out.1), custom_call_target="tpu_custom_call" | custom-call | tf_op jit(solution)/shard_map/pallas_call | solution.py:199
  70.7 2.3 %copy.6 = bf16[2,1024,256]{2,1,0:T(8,128)(2,1)} copy(bf16[2,1024,256]{2,1,0:T(8,128)(2,1)} %shard_map.46) | data formatting | bytes 2097152
